TPU v7x, 32 devices: a whole 2x2x4 slice. The times are simulated.
32 devices in a mesh: shard: 4 (over z), ctx: 2 (over x), tp: 4 (over y, core).
Axes of the slice: x: 2, y: 2, z: 4, core: 2. Of those that a mesh axis runs over, the one named last changes fastest.
Arguments:
- activations: bfloat16 [4, 1040, 768], P('shard', 'ctx'), may hold values from -6 to 6
- slot_counts: int32 [4, 2], P('shard'), may hold values from 1 to 520, as said below
- qkv_weight: bfloat16 [3, 768, 768], P(None, 'shard', 'tp'), may hold values from -0.21875 to 0.21875
- proj_weight: bfloat16 [768, 768], P('tp', 'shard'), may hold values from -3 to 3
- up_weight: bfloat16 [768, 3072], P('shard', 'tp'), may hold values from -0.21875 to 0.21875
- down_weight: bfloat16 [3072, 768], P('tp', 'shard'), may hold values from -0.109375 to 0.109375
- norm_gains: bfloat16 [2, 768], P(None, 'shard'), may hold values from 0.5 to 1.5
- row_biases: bfloat16 [4, 768], P(None, 'shard'), may hold values from -3 to 3
- head_biases: bfloat16 [2, 768], P(None, 'tp'), may hold values from -0.59765625 to 0.59765625
- hidden_bias: bfloat16 [3072], P('tp'), may hold values from -3 to 3
- cotangent: bfloat16 [4, 1040, 768], P('shard', 'ctx'), may hold values from -6 to 6
Outputs:
- layer_out: bfloat16 [4, 1040, 768], P('shard', ('ctx', 'tp'))
- input_grad: bfloat16 [4, 1040, 768], P('shard', ('ctx', 'tp'))
- qkv_weight_grad: float32 [3, 768, 768], P(None, 'shard', 'tp')
- proj_weight_grad: float32 [768, 768], P('tp', 'shard')
- up_weight_grad: float32 [768, 3072], P('shard', 'tp')
- down_weight_grad: float32 [3072, 768], P('tp', 'shard')
- norm_gains_grad: float32 [2, 768], P(None, 'shard')
- row_biases_grad: float32 [4, 768], P(None, 'shard')
- head_biases_grad: float32 [2, 768], P(None, 'tp')
- hidden_bias_grad: float32 [3072], P('tp')
Inputs may be any that keep to these rules, and one draw needn't show every extreme that they name: Row b splits image b's 1025 tokens over the indices of ctx: slot_counts[b, r] of them lie in the first slots of index r's 520; each row sums to 1025; in each row one index holds exactly 520 and the others share the rest as evenly as possible.
All inputs are finite; a program needn't handle non-finite values.
Results may differ from a plain program's by a relative error of at most 0.012.
Values may be sent and summed in bfloat16 or wider, within the bound.
No kernel may reach another device: no remote copies, remote signals or barrier semaphores. Data moves between devices by JAX's collectives and lax.ppermute only.
A program may use at most 64 MiB of HBM per device.

v0:
```python
import math
import jax
import jax.numpy as jnp
from jax import lax
from jax.sharding import PartitionSpec as P

HD = 64
EPS = 1e-06
NEG = -1e30


def layer_norm(values, gain, shift):
    centred = values - jnp.mean(values, axis=-1, keepdims=True)
    spread = jnp.mean(centred * centred, axis=-1, keepdims=True)
    return centred * lax.rsqrt(spread + EPS) * gain + shift


def exact_gelu(hidden):
    return jax.nn.gelu(hidden, approximate=False)


def head_scores(queries, keys, keep):
    scale = 1.0 / math.sqrt(HD)
    scores = jnp.einsum("qhd,khd->hqk", queries, keys, preferred_element_type=jnp.float32) * scale
    return jnp.where(keep[None, None, :], scores, NEG)


def attend(item):
    queries, keys, values, keep = item
    slot_total = queries.shape[0]
    query_heads = queries.reshape(slot_total, -1, HD)
    key_heads = keys.reshape(keys.shape[0], -1, HD)
    value_heads = values.reshape(values.shape[0], -1, HD)
    scores = head_scores(query_heads, key_heads, keep)
    peak = jnp.max(scores, axis=-1, keepdims=True)
    log_total = peak + jnp.log(jnp.sum(jnp.exp(scores - peak), axis=-1, keepdims=True))
    attn_weights = jnp.exp(scores - log_total).astype(jnp.bfloat16)
    mixed = jnp.einsum(
        "hqk,khd->qhd", attn_weights, value_heads, preferred_element_type=jnp.float32
    )
    return (mixed.reshape(slot_total, -1).astype(jnp.bfloat16), log_total)


def attend_back(item):
    queries, keys, values, keep, log_total, grad_mixed = item
    scale = 1.0 / math.sqrt(HD)
    slot_total = queries.shape[0]
    key_total = keys.shape[0]
    query_heads = queries.reshape(slot_total, -1, HD)
    key_heads = keys.reshape(key_total, -1, HD)
    value_heads = values.reshape(key_total, -1, HD)
    grad_heads = grad_mixed.reshape(slot_total, -1, HD)
    scores = head_scores(query_heads, key_heads, keep)
    attn_weights = jnp.exp(scores - log_total)
    weights_low = attn_weights.astype(jnp.bfloat16)
    grad_weights = jnp.einsum(
        "qhd,khd->hqk", grad_heads, value_heads, preferred_element_type=jnp.float32
    )
    grad_values = jnp.einsum(
        "hqk,qhd->khd", weights_low, grad_heads, preferred_element_type=jnp.float32
    )
    inner = jnp.sum(grad_weights * attn_weights, axis=-1, keepdims=True)
    grad_scores = (attn_weights * (grad_weights - inner)).astype(jnp.bfloat16)
    grad_queries = (
        jnp.einsum("hqk,khd->qhd", grad_scores, key_heads, preferred_element_type=jnp.float32)
        * scale
    )
    grad_keys = (
        jnp.einsum("hqk,qhd->khd", grad_scores, query_heads, preferred_element_type=jnp.float32)
        * scale
    )
    return (
        grad_queries.reshape(slot_total, -1),
        grad_keys.reshape(key_total, -1),
        grad_values.reshape(key_total, -1),
    )


def per_device(
    activations,
    slot_counts,
    qkv_weight,
    proj_weight,
    up_weight,
    down_weight,
    norm_gains,
    row_biases,
    head_biases,
    hidden_bias,
    cotangent,
):
    images, slots, width = activations.shape
    n_ctx = lax.axis_size("ctx")
    n_tp = lax.axis_size("tp")
    row_count = images * slots
    quarter = row_count // n_tp
    row_start = lax.axis_index("tp") * quarter

    def own_rows(values):
        return lax.dynamic_slice_in_dim(values, row_start, quarter, 0)

    gathered = (
        lax.all_gather(qkv_weight, "shard", axis=1, tiled=True),
        lax.all_gather(proj_weight, "shard", axis=1, tiled=True),
        lax.all_gather(up_weight, "shard", axis=0, tiled=True),
        lax.all_gather(down_weight, "shard", axis=1, tiled=True),
        lax.all_gather(norm_gains, "shard", axis=1, tiled=True),
        lax.all_gather(row_biases, "shard", axis=1, tiled=True),
    )
    qkv_full, proj_full, up_full, down_full, gains_full, shifts_full = gathered
    gains = gains_full.astype(jnp.float32)
    shifts = shifts_full.astype(jnp.float32)
    ctx_rank = lax.axis_index("ctx")
    rank_ids = jnp.arange(n_ctx, dtype=jnp.int32)
    own_count = jnp.sum(jnp.where(rank_ids[None, :] == ctx_rank, slot_counts, 0), axis=1)
    slot_ids = jnp.arange(slots, dtype=jnp.int32)
    row_valid = (slot_ids[None, :] < own_count[:, None]).reshape(row_count, 1)
    share_valid = own_rows(row_valid)
    key_valid = jnp.repeat(slot_counts, slots, axis=1) > jnp.tile(slot_ids, n_ctx)[None, :]
    act_in = activations.reshape(row_count, width).astype(jnp.float32)
    normed, norm_one_back = jax.vjp(layer_norm, act_in, gains[0], shifts[0])
    normed_low = normed.astype(jnp.bfloat16)
    projected = jnp.einsum("rd,kde->kre", normed_low, qkv_full, preferred_element_type=jnp.float32)
    biases = head_biases.astype(jnp.float32)
    queries = (projected[0] + biases[0]).astype(jnp.bfloat16).reshape(images, slots, -1)
    keys = projected[1].astype(jnp.bfloat16).reshape(images, slots, -1)
    values = (projected[2] + biases[1]).astype(jnp.bfloat16).reshape(images, slots, -1)
    keys_all, values_all = (
        lax.all_gather(keys, "ctx", axis=1, tiled=True),
        lax.all_gather(values, "ctx", axis=1, tiled=True),
    )
    mixed, log_totals = lax.map(attend, (queries, keys_all, values_all, key_valid))
    mixed_flat = mixed.reshape(row_count, -1)
    attn_part = jnp.dot(mixed_flat, proj_full, preferred_element_type=jnp.float32)
    attn_sum = lax.psum(attn_part, "tp")
    middle_full = act_in + attn_sum + shifts[2]
    normed_two, norm_two_back = jax.vjp(layer_norm, middle_full, gains[1], shifts[1])
    normed_two_low = normed_two.astype(jnp.bfloat16)
    middle = own_rows(middle_full)
    hidden = jnp.dot(
        normed_two_low, up_full, preferred_element_type=jnp.float32
    ) + hidden_bias.astype(jnp.float32)
    gelu_out, gelu_back = jax.vjp(exact_gelu, hidden)
    gelu_low = gelu_out.astype(jnp.bfloat16)
    mlp_part = jnp.dot(gelu_low, down_full, preferred_element_type=jnp.float32)
    mlp_sum = own_rows(lax.psum(mlp_part.astype(jnp.bfloat16), "tp").astype(jnp.float32))
    layer_out = (
        jnp.where(share_valid, middle + mlp_sum + shifts[3], 0.0)
        .astype(jnp.bfloat16)
        .reshape(images, quarter, width)
    )
    qkv_use, proj_use, up_use, down_use = (qkv_full, proj_full, up_full, down_full)
    grad_out = jnp.where(row_valid, cotangent.reshape(row_count, width).astype(jnp.float32), 0.0)
    grad_branch = grad_out.astype(jnp.bfloat16)
    down_grad = jnp.einsum("rf,rd->fd", gelu_low, grad_branch, preferred_element_type=jnp.float32)
    grad_gelu = jnp.einsum("rd,fd->rf", grad_branch, down_use, preferred_element_type=jnp.float32)
    (grad_hidden,) = gelu_back(grad_gelu)
    grad_hidden_low = grad_hidden.astype(jnp.bfloat16)
    up_grad = jnp.einsum(
        "rd,rf->df", normed_two_low, grad_hidden_low, preferred_element_type=jnp.float32
    )
    hidden_grad = jnp.sum(grad_hidden_low.astype(jnp.float32), axis=0)
    grad_normed_part = jnp.einsum(
        "rf,df->rd", grad_hidden_low, up_use, preferred_element_type=jnp.float32
    )
    grad_normed_two = lax.psum(grad_normed_part, "tp")
    grad_middle_norm, gain_two_grad, shift_two_grad = norm_two_back(grad_normed_two)
    grad_middle_full = grad_out + grad_middle_norm
    grad_attn = grad_middle_full.astype(jnp.bfloat16)
    grad_middle = own_rows(grad_middle_full)
    proj_grad = jnp.einsum("re,rd->ed", mixed_flat, grad_attn, preferred_element_type=jnp.float32)
    grad_mixed = (
        jnp.einsum("rd,ed->re", grad_attn, proj_use, preferred_element_type=jnp.float32)
        .astype(jnp.bfloat16)
        .reshape(images, slots, -1)
    )
    grad_queries, grad_keys_part, grad_values_part = lax.map(
        attend_back, (queries, keys_all, values_all, key_valid, log_totals, grad_mixed)
    )
    grad_keys, grad_values = (
        lax.psum_scatter(grad_keys_part, "ctx", scatter_dimension=1, tiled=True),
        lax.psum_scatter(grad_values_part, "ctx", scatter_dimension=1, tiled=True),
    )
    stacked = jnp.stack(
        [
            grad_queries.reshape(row_count, -1),
            grad_keys.reshape(row_count, -1),
            grad_values.reshape(row_count, -1),
        ]
    ).astype(jnp.bfloat16)
    qkv_grad = jnp.einsum("rd,kre->kde", normed_low, stacked, preferred_element_type=jnp.float32)
    stacked_wide = stacked.astype(jnp.float32)
    head_grad = jnp.stack([jnp.sum(stacked_wide[0], axis=0), jnp.sum(stacked_wide[2], axis=0)])
    grad_normed_one_part = jnp.einsum(
        "kre,kde->rd", stacked, qkv_use, preferred_element_type=jnp.float32
    )
    grad_normed_one = lax.psum(grad_normed_one_part, "tp")
    grad_input_norm_full, gain_one_grad, shift_one_grad = norm_one_back(grad_normed_one)
    grad_input_norm = own_rows(grad_input_norm_full)
    gains_grad = jnp.stack([gain_one_grad, gain_two_grad])
    norm_shift_grads = jnp.stack([shift_one_grad, shift_two_grad])
    input_grad = (
        (grad_middle + grad_input_norm).astype(jnp.bfloat16).reshape(images, quarter, width)
    )
    shifts_grad = jnp.concatenate(
        [
            norm_shift_grads,
            jnp.stack(
                [
                    jnp.sum(grad_attn.astype(jnp.float32), axis=0),
                    jnp.sum(grad_branch.astype(jnp.float32), axis=0),
                ]
            ),
        ],
        axis=0,
    )
    summed = lax.psum((qkv_grad, proj_grad, up_grad, down_grad, gains_grad, shifts_grad), "ctx")
    owned = (
        lax.psum_scatter(summed[0], "shard", scatter_dimension=1, tiled=True),
        lax.psum_scatter(summed[1], "shard", scatter_dimension=1, tiled=True),
        lax.psum_scatter(summed[2], "shard", scatter_dimension=0, tiled=True),
        lax.psum_scatter(summed[3], "shard", scatter_dimension=1, tiled=True),
        lax.psum_scatter(summed[4], "shard", scatter_dimension=1, tiled=True),
        lax.psum_scatter(summed[5], "shard", scatter_dimension=1, tiled=True),
    )
    bias_totals = lax.psum((head_grad, hidden_grad), ("shard", "ctx"))
    return (
        layer_out,
        input_grad,
        owned[0],
        owned[1],
        owned[2],
        owned[3],
        owned[4],
        owned[5],
        bias_totals[0],
        bias_totals[1],
    )


def solution(mesh):
    placed = (
        P("shard", "ctx", None),
        P("shard", None),
        P(None, "shard", "tp"),
        P("tp", "shard"),
        P("shard", "tp"),
        P("tp", "shard"),
        P(None, "shard"),
        P(None, "shard"),
        P(None, "tp"),
        P("tp"),
        P("shard", "ctx", None),
    )
    return jax.shard_map(
        per_device,
        mesh=mesh,
        in_specs=placed,
        out_specs=(
            P("shard", ("ctx", "tp"), None),
            P("shard", ("ctx", "tp"), None),
            P(None, "shard", "tp"),
            P("tp", "shard"),
            P("shard", "tp"),
            P("tp", "shard"),
            P(None, "shard"),
            P(None, "shard"),
            P(None, "tp"),
            P("tp"),
        ),
        check_vma=False,
    )
```

profile of v0, /device:TPU:0, one launch (start us, length us, event | category | flops | bytes accessed | tf_op | source)
XLA Modules:
  0.0 542.7 jit_solution(16820646463041530862)
XLA Ops:
  10.4 12.8 %all-gather = bf16[4,192,2]{1,2,0:T(2,128)(2,1)S(1)} all-gather(bf16[1,192,2]{1,2,0:T(2,128)(2,1)} %bitcast.183), channel_id=1, replica_groups=mesh['shard'=4,'ctx'=2,'tp'=4] {'shard'}, dimensions={0}, use_global_device_ids=true | all-gather | bytes 3840 | tf_op jit(solution)/shard_map/all_gather | solution.py:107
  26.3 11.9 %all-gather.1 = bf16[4,192,4]{1,2,0:T(4,128)(2,1)S(1)} all-gather(bf16[1,192,4]{1,2,0:T(4,128)(2,1)S(1)} %bitcast.182), channel_id=1, replica_groups=mesh['shard'=4,'ctx'=2,'tp'=4] {'shard'}, dimensions={0}, use_global_device_ids=true | all-gather | bytes 7680 | tf_op jit(solution)/shard_map/all_gather | solution.py:108
  38.4 15.8 %all_gather.29 = bf16[192,768]{0,1:T(8,128)(2,1)} all-gather(bf16[192,192]{0,1:T(8,128)(2,1)S(1)} %copy.48), channel_id=1, replica_groups=mesh['shard'=4,'ctx'=2,'tp'=4] {'shard'}, dimensions={1}, use_global_device_ids=true | all-gather | bytes 368640 | tf_op jit(solution)/shard_map/all_gather | solution.py:104
  54.5 22.9 %all_gather.26 = bf16[3,768,192]{2,0,1:T(4,128)(2,1)S(1)} all-gather(bf16[3,192,192]{2,0,1:T(4,128)(2,1)S(1)} %copy.42), channel_id=1, replica_groups=mesh['shard'=4,'ctx'=2,'tp'=4] {'shard'}, dimensions={1}, use_global_device_ids=true | all-gather | bytes 1105920 | tf_op jit(solution)/shard_map/all_gather | solution.py:103
  81.4 11.9 %all_gather.28 = bf16[1,1040,192]{2,0,1:T(2,128)(2,1)S(1)} all-gather(bf16[1,520,192]{2,0,1:T(2,128)(2,1)S(1)} %copy.46), channel_id=1, replica_groups=mesh['shard'=4,'ctx'=2,'tp'=4] {'ctx'}, dimensions={1}, use_global_device_ids=true | all-gather | bytes 599040 | tf_op jit(solution)/shard_map/all_gather | solution.py:129
  93.3 2.6 copy.47
  95.9 1.8 copy.44
  97.7 9.9 %all_gather.27 = bf16[1,1040,192]{2,0,1:T(2,128)(2,1)S(1)} all-gather(bf16[1,520,192]{2,0,1:T(2,128)(2,1)S(1)} %copy.44), channel_id=1, replica_groups=mesh['shard'=4,'ctx'=2,'tp'=4] {'ctx'}, dimensions={1}, use_global_device_ids=true | all-gather | bytes 599040 | tf_op jit(solution)/shard_map/all_gather | solution.py:130
  107.7 2.6 copy.45
  120.6 39.9 %all-reduce.9.cloned.1.call-done = f32[520,768]{1,0:T(8,128)} async-done(((f32[520,768]{1,0:T(8,128)}), f32[520,768]{1,0:T(8,128)}) %all-reduce.9.cloned.1.call-update) | async-done | bytes 1597456 | tf_op jit(solution)/shard_map/psum | solution.py:135
  162.6 6.9 %multiply_convert_fusion.1 = (bf16[520,768]{1,0:T(8,128)(2,1)}, f32[520,768]{1,0:T(8,128)}, f32[520,768]{1,0:T(8,128)}) fusion(f32[768]{0:T(1024)S(1)} %convert_element_type.113, bf16[768,768]{1,0:T(8,128)(2,1)} %all-gather.5.cloned.1.call-done, f32[520,768]{1,0:T(8,128)S(1)} %get-tuple-element.132, f32[768]{0:T(1024)S(1)} %get-tuple-element.110, ...), kind=kOutput, calls=%fused_computation.36 | convolution fusion | flops 641771520 | bytes 6784064 | tf_op jit(solution)/shard_map/dot_general | solution.py:140
  169.6 10.6 %all-gather.7.cloned.1.call-done = bf16[768,768]{0,1:T(8,128)(2,1)} async-done(((bf16[768,192]{0,1:T(8,128)(2,1)}), bf16[768,768]{0,1:T(8,128)(2,1)}) %all-gather.7.cloned.1.call-update) | async-done | bytes 1179664 | tf_op jit(solution)/shard_map/all_gather | solution.py:106
  180.2 3.8 convert_reduce_fusion.1
  184.9 2.0 fusion.58
  186.9 42.7 %all-reduce.13.cloned.1.call-done = f32[520,768]{1,0:T(8,128)} async-done(((f32[520,768]{1,0:T(8,128)}), f32[520,768]{1,0:T(8,128)}) %all-reduce.13.cloned.1.call-update) | async-done | bytes 1597456 | tf_op jit(solution)/shard_map/psum | solution.py:166
  229.6 2.3 multiply_reduce_fusion.1
  231.9 2.2 fusion.51
  236.3 2.5 fusion.24
  238.8 4.8 multiply_reduce_fusion
  243.6 3.7 copy.53
  247.3 2.3 copy.68
  249.7 6.0 %multiply_convert_fusion = bf16[3,520,1040]{2,1,0:T(8,128)(2,1)S(1)} fusion(f32[3,520,1040]{2,1,0:T(8,128)} %get-tuple-element.140, f32[3,520,1040]{2,1,0:T(8,128)} %copy-done, f32[3,520]{1,0:T(4,128)S(1)} %get-tuple-element.139, f32[3,520]{1,0:T(4,128)S(1)} %log_add_fusion), kind=kLoop, calls=%fused_computation | loop fusion | flops 6489600 | bytes 16236480 | tf_op jit(solution)/shard_map/while/body/eval_jaxpr/convert_element_type | solution.py:63
  255.7 2.1 convolution_multiply_fusion
  257.8 3.3 copy.51
  262.4 3.4 fusion.23
  265.8 4.5 reduce-scatter.27.cloned.1.call-done
  272.6 20.4 %reduce-scatter.25.cloned.1.call-done = f32[520,192]{1,0:T(8,128)} async-done(((f32[1040,192]{1,0:T(8,128)}), f32[520,192]{1,0:T(8,128)}) %reduce-scatter.25.cloned.1.call-update) | async-done | bytes 399376
  295.8 3.4 convolution_bitcast_fusion.1
  300.2 2.9 convolution_bitcast_fusion.2
  303.1 2.4 convolution_bitcast_fusion
  305.5 4.2 copy.55
  309.7 4.7 reshape.243
  314.6 4.1 fusion.48
  318.7 4.1 fusion.39
  322.8 3.2 convolution_convert_fusion
  326.2 16.6 %all-reduce.15.cloned.1.call-done = f32[520,768]{1,0:T(8,128)} async-done(((f32[520,768]{1,0:T(8,128)}), f32[520,768]{1,0:T(8,128)}) %all-reduce.15.cloned.1.call-update) | async-done | bytes 1597456 | tf_op jit(solution)/shard_map/psum | solution.py:197
  342.8 2.2 fusion.11
  347.1 1.7 copy.58
  348.8 20.7 %reduce-scatter.29.cloned.1.call-done = f32[192,576]{1,0:T(8,128)} async-done(((f32[768,576]{1,0:T(8,128)}), f32[192,576]{1,0:T(8,128)}) %reduce-scatter.29.cloned.1.call-update) | async-done | bytes 442384
  372.0 46.6 %reduce-scatter.21.cloned.1.call-done = f32[192,768]{1,0:T(8,128)} async-done(((f32[768,768]{1,0:T(8,128)}), f32[192,768]{1,0:T(8,128)}) %reduce-scatter.21.cloned.1.call-update) | async-done | bytes 589840 | tf_op jit(solution)/shard_map/reduce_scatter | solution.py:221
  418.6 49.6 %reduce-scatter.23.cloned.1.call-done = f32[768,192]{0,1:T(8,128)} async-done(((f32[768,768]{0,1:T(8,128)}), f32[768,192]{0,1:T(8,128)}) %reduce-scatter.23.cloned.1.call-update) | async-done | bytes 589840 | tf_op jit(solution)/shard_map/reduce_scatter | solution.py:222
  468.9 1.8 fusion.31
  471.0 21.1 %all-reduce = (f32[2,192]{1,0:T(2,128)}, f32[768]{0:T(1024)}) all-reduce(f32[2,192]{1,0:T(2,128)S(1)} %pad_maximum_fusion.3, f32[768]{0:T(1024)S(1)} %get-tuple-element.141), channel_id=1, replica_groups=mesh['shard'=4,'ctx'=2,'tp'=4] {'shard','ctx'}, use_global_device_ids=true, to_apply=%region_38.39 | all-reduce | flops 1152 | bytes 9216 | tf_op jit(solution)/shard_map/psum | solution.py:226
  493.0 1.8 fusion.32
  495.8 17.1 %reduce-scatter.35.cloned.1.call-done = f32[192,4]{1,0:T(8,128)} async-done(((f32[768,4]{1,0:T(8,128)}), f32[192,4]{1,0:T(8,128)}) %reduce-scatter.35.cloned.1.call-update) | async-done | bytes 3088
  513.8 5.7 %all-reduce.1 = (f32[2,192]{1,0:T(2,128)}, f32[4,192]{1,0:T(4,128)}) all-reduce(f32[2,192]{1,0:T(2,128)S(1)} %copy.60, f32[4,192]{1,0:T(4,128)S(1)} %copy.62), channel_id=1, replica_groups=mesh['shard'=4,'ctx'=2,'tp'=4] {'ctx'}, use_global_device_ids=true, to_apply=%region_28.29 | all-reduce | flops 1152 | bytes 9216 | tf_op jit(solution)/shard_map/psum | solution.py:217
  519.5 10.2 %all-reduce.17.cloned.1.call-done = (f32[3,192,192]{1,2,0:T(8,128)}, f32[192,192]{1,0:T(8,128)}, f32[192,768]{1,0:T(8,128)}, f32[768,192]{0,1:T(8,128)}) async-done(((f32[3,192,192]{1,2,0:T(8,128)}, f32[192,192]{1,0:T(8,128)}, f32[192,768]{1,0:T(8,128)}, f32[768,192]{0,1:T(8,128)}), (f32[3,192,192]{1,2,0:T(8,128)}, f32[192,192]{1,0:T(8,128)}, f32[192,768]{1,0:T(8,128)}, ...) | async-done | bytes 1769488 | tf_op jit(solution)/shard_map/psum | solution.py:217
  529.8 2.2 copy.50
  (158 shorter events, 44.3 us)
Async XLA Ops:
  8.0 18.3 %copy-start.20 = (bf16[4,192]{1,0:T(4,128)(2,1)S(1)}, bf16[4,192]{1,0:T(4,128)(2,1)}, u32[]{:S(2)}) copy-start(bf16[4,192]{1,0:T(4,128)(2,1)} %param.18) | copy-start | bytes 4612
  8.0 30.3 %copy-start.19 = (bf16[192,192]{1,0:T(8,128)(2,1)S(1)}, bf16[192,192]{1,0:T(8,128)(2,1)}, u32[]{:S(2)}) copy-start(bf16[192,192]{1,0:T(8,128)(2,1)} %param.14) | copy-start | bytes 221188
  8.0 46.2 %copy-start.18 = (bf16[3,192,192]{2,1,0:T(8,128)(2,1)S(1)}, bf16[3,192,192]{2,1,0:T(8,128)(2,1)}, u32[]{:S(2)}) copy-start(bf16[3,192,192]{2,1,0:T(8,128)(2,1)} %param.13) | copy-start | bytes 663556
  8.0 152.5 %all-reduce.9.cloned.1.call-start = ((), (), s32[]{:S(2)}) async-start(), calls=%async_computation.8 | async-start | bytes 3194880 | tf_op jit(solution)/shard_map/psum | solution.py:135
  77.4 1.1 copy-start.2
  78.3 1.3 copy-start.14
  95.9 14.4 %copy-start.5 = (bf16[1,1040,192]{1,2,0:T(8,128)(2,1)}, bf16[1,1040,192]{1,2,0:T(8,128)(2,1)S(1)}, u32[]{:S(2)}) copy-start(bf16[1,1040,192]{1,2,0:T(8,128)(2,1)S(1)} %copy.47) | copy-start | bytes 1198084
  111.9 3.0 copy-start
  114.8 1.4 copy-start.6
  116.2 1.7 copy-start.8
  117.9 1.4 copy-start.22
  117.9 2.7 copy-start.21
  117.9 44.7 %all-gather.5.cloned.1.call-start = ((), (), s32[]{:S(2)}) async-start(), calls=%async_computation.9 | async-start | bytes 1474560 | tf_op jit(solution)/shard_map/all_gather | solution.py:105
  118.5 61.7 %all-gather.7.cloned.1.call-start = ((), (), s32[]{:S(2)}) async-start(), calls=%async_computation.10 | async-start | bytes 1474560 | tf_op jit(solution)/shard_map/all_gather | solution.py:106
  119.1 110.5 %all-reduce.13.cloned.1.call-start = ((), (), s32[]{:S(2)}) async-start(), calls=%async_computation.12 | async-start | bytes 3194880 | tf_op jit(solution)/shard_map/psum | solution.py:166
  180.2 4.7 copy-start.23
  184.0 0.9 copy-start.24
  186.9 83.4 %reduce-scatter.27.cloned.1.call-start = ((), (), s32[]{:S(2)}) async-start(), calls=%async_computation.17 | async-start | bytes 1597440
  229.6 6.7 %slice-start = ((s8[7188480]{0:T(1024)(128)(4,1)}), s8[4194304]{0:T(1024)(128)(4,1)S(1)}, s32[]{:S(2)}) async-start(s8[7188480]{0:T(1024)(128)(4,1)} %bitcast.146), calls=%async_computation.23 | async-start | bytes 8388608
  231.9 2.3 copy-start.15
  231.9 4.4 slice-start.1
  234.1 1.6 copy-start.7
  234.6 1.2 copy-start.3
  249.7 43.4 %reduce-scatter.25.cloned.1.call-start = ((), (), s32[]{:S(2)}) async-start(), calls=%async_computation.16 | async-start | bytes 1597440
  255.7 2.1 copy-start.1
  262.1 80.6 %all-reduce.15.cloned.1.call-start = ((), (), s32[]{:S(2)}) async-start(), calls=%async_computation.13 | async-start | bytes 3194880 | tf_op jit(solution)/shard_map/psum | solution.py:197
  272.6 30.5 %copy-start.10 = (bf16[1,520,192]{1,2,0:T(8,128)(2,1)}, bf16[1,520,192]{1,2,0:T(8,128)(2,1)S(1)}, u32[]{:S(2)}) copy-start(bf16[1,520,192]{1,2,0:T(8,128)(2,1)S(1)} %copy.54) | copy-start | bytes 599044
  299.2 0.9 copy-start.9
  299.2 3.9 copy-start.12
  299.2 47.8 %reduce-scatter.31.cloned.1.call-start = ((), (), s32[]{:S(2)}) async-start(), calls=%async_computation.19 | async-start | bytes 983040
  303.0 66.4 %reduce-scatter.29.cloned.1.call-start = ((), (), s32[]{:S(2)}) async-start(), calls=%async_computation.18 | async-start | bytes 2457600
  314.5 104.1 %reduce-scatter.21.cloned.1.call-start = ((), (), s32[]{:S(2)}) async-start(), calls=%async_computation.14 | async-start | bytes 2949120 | tf_op jit(solution)/shard_map/reduce_scatter | solution.py:221
  318.6 149.6 %reduce-scatter.23.cloned.1.call-start = ((), (), s32[]{:S(2)}) async-start(), calls=%async_computation.15 | async-start | bytes 2949120 | tf_op jit(solution)/shard_map/reduce_scatter | solution.py:222
  322.8 146.1 %all-reduce.11.cloned.1.call-start = ((), (), s32[]{:S(2)}) async-start(), calls=%async_computation.11 | async-start | bytes 1597440 | tf_op jit(solution)/shard_map/psum | solution.py:146
  326.1 168.7 %reduce-scatter.33.cloned.1.call-start = ((), (), s32[]{:S(2)}) async-start(), calls=%async_computation.20 | async-start | bytes 491520
  346.0 166.9 %reduce-scatter.35.cloned.1.call-start = ((), (), s32[]{:S(2)}) async-start(), calls=%async_computation.21 | async-start | bytes 491520
  347.0 182.7 %all-reduce.17.cloned.1.call-start = ((), (), s32[]{:S(2)}) async-start(), calls=%async_computation.22 | async-start | bytes 3932160 | tf_op jit(solution)/shard_map/psum | solution.py:217
  372.0 98.7 %copy-start.11 = (bf16[1,520,192]{1,2,0:T(8,128)(2,1)S(1)}, bf16[1,520,192]{1,2,0:T(8,128)(2,1)}, u32[]{:S(2)}) copy-start(bf16[1,520,192]{1,2,0:T(8,128)(2,1)} %copy-done.10) | copy-start | bytes 599044
  372.0 98.7 %copy-start.13 = (bf16[1,520,192]{1,2,0:T(8,128)(2,1)S(1)}, bf16[1,520,192]{1,2,0:T(8,128)(2,1)}, u32[]{:S(2)}) copy-start(bf16[1,520,192]{1,2,0:T(8,128)(2,1)} %copy.52) | copy-start | bytes 599044
  470.7 21.5 %copy-start.4 = (f32[520,768]{1,0:T(8,128)S(1)}, f32[520,768]{1,0:T(8,128)}, u32[]{:S(2)}) copy-start(f32[520,768]{1,0:T(8,128)} %all-reduce.15.cloned.1.call-done) | copy-start | bytes 4792324
  529.7 3.8 copy-start.17
  529.8 4.7 copy-start.16
Sparse Core Ops, SparseCore 0:
  118.0 42.4 all-reduce.8
  187.0 42.5 all-reduce.12
  249.8 20.4 reduce-scatter.26
  272.5 20.4 reduce-scatter.24
  299.4 43.3 all-reduce.14
  345.0 34.5 all-reduce.10
  468.3 61.3 all-reduce.16
Sparse Core Ops, SparseCore 1:
  120.0 29.3 all-gather.4
  150.7 29.4 all-gather.6
  303.1 23.0 reduce-scatter.30
  328.5 40.9 reduce-scatter.28
  371.8 46.7 reduce-scatter.20
  420.9 47.2 reduce-scatter.22
  471.0 20.1 reduce-scatter.32
  493.9 18.9 reduce-scatter.34
where the time goes:
time: 544 us; the launch traced here: 543 us
  waiting for transfers between devices  280 us (51%)
  blocking collectives  112 us (21%)
  local copies, waits for them, and re-layouts  53.1 us (10%)
  matrix products  51.7 us (10%)
  other arithmetic  28.1 us (5%)
  between operations  16.2 us (3%)
    unnamed x21, waiting for transfers between devices  63.9 us
    reduce_scatter x1, waiting for transfers between devices, per_device(): lax.psum_scatter(summed[3], 'shard', scatter_dimension=1, tiled=True)  49.6 us
    reduce_scatter x1, waiting for transfers between devices, per_device(): lax.psum_scatter(summed[2], 'shard', scatter_dimension=0, tiled=True)  46.6 us
    unnamed x77, local copies, waits for them, and re-layouts  43 us
    psum x1, waiting for transfers between devices, per_device(): grad_normed_two = lax.psum(grad_normed_part, 'tp')  42.7 us
    psum x1, waiting for transfers between devices, per_device(): attn_sum = lax.psum(attn_part, 'tp')  39.9 us
    all_gather x1, blocking collectives, per_device(): lax.all_gather(qkv_weight, 'shard', axis=1, tiled=True)  22.9 us
    psum x1, blocking collectives, per_device(): bias_totals = lax.psum((head_grad, hidden_grad), ('shard', 'ctx'))  21.1 us
  transfers between devices with their start and end apart: 15, of which 11 were waited for; matrix products, arithmetic and copies ran while one was open for 13% of the time, Pallas kernels for 0%

commit v1 on v0

--- a/solution.py
+++ b/solution.py
@@ -7,6 +7,28 @@
 HD = 64
 EPS = 1e-06
 NEG = -1e30
+
+
+def laid_out(blocks, dim):
+    blocks = jnp.moveaxis(blocks, 0, dim)
+    shape = blocks.shape
+    return blocks.reshape(*shape[:dim], shape[dim] * shape[dim + 1], *shape[dim + 2 :])
+
+
+def collect(value, axis, dim):
+    size = lax.axis_size(axis)
+    pairs = [(i, (i + 1) % size) for i in range(size)]
+    back = [(b, a) for a, b in pairs]
+    lower, upper = ([], [])
+    for lap in range(size - 1):
+        if lap % 2 == 0:
+            lower.append(lax.ppermute(lower[-1] if lower else value, axis, pairs))
+        else:
+            upper.append(lax.ppermute(upper[-1] if upper else value, axis, back))
+    parts = jnp.stack([*lower[::-1], value, *upper])
+    shift = lax.axis_index(axis) - len(lower)
+    parts = parts[(jnp.arange(size) - shift) % size]
+    return laid_out(parts, dim)
 
 
 def layer_norm(values, gain, shift):
@@ -104,7 +126,7 @@
         lax.all_gather(proj_weight, "shard", axis=1, tiled=True),
         lax.all_gather(up_weight, "shard", axis=0, tiled=True),
         lax.all_gather(down_weight, "shard", axis=1, tiled=True),
-        lax.all_gather(norm_gains, "shard", axis=1, tiled=True),
+        collect(norm_gains, "shard", 1),
         lax.all_gather(row_biases, "shard", axis=1, tiled=True),
     )
     qkv_full, proj_full, up_full, down_full, gains_full, shifts_full = gathered

time: 544 us -> 542 us (level)
  blocking collectives: 112 us -> 102 us
    all_gather x1 -> x0, blocking collectives: 12.8 us -> none  [per_device(): lax.all_gather(norm_gains, 'shard', axis=1, tiled=True)]
    unnamed x77 -> x81, local copies, waits for them, and re-layouts: 43 us -> 42.7 us
  transfers between devices with their start and end apart: 15 -> 18, of which waited for: 11 -> 11; matrix products, arithmetic and copies ran while one was open for 13% -> 14% of each run, Pallas kernels for 0% -> 0%
where the time goes in v1:
time: 542 us; the launch traced here: 540 us
  waiting for transfers between devices  283 us (52%)
  blocking collectives  102 us (19%)
  local copies, waits for them, and re-layouts  52.8 us (10%)
  matrix products  51.7 us (10%)
  other arithmetic  28.2 us (5%)
  between operations  16.3 us (3%)
  starting transfers between devices  6.27 us (1%)
    unnamed x21, waiting for transfers between devices  63.9 us
    reduce_scatter x1, waiting for transfers between devices, per_device(): lax.psum_scatter(summed[3], 'shard', scatter_dimension=1, tiled=True)  49.4 us
    reduce_scatter x1, waiting for transfers between devices, per_device(): lax.psum_scatter(summed[2], 'shard', scatter_dimension=0, tiled=True)  46.8 us
    psum x1, waiting for transfers between devices, per_device(): attn_sum = lax.psum(attn_part, 'tp')  43 us
    unnamed x81, local copies, waits for them, and re-layouts  42.7 us
    psum x1, waiting for transfers between devices, per_device(): grad_normed_two = lax.psum(grad_normed_part, 'tp')  42.7 us
    all_gather x1, blocking collectives, per_device(): lax.all_gather(qkv_weight, 'shard', axis=1, tiled=True)  26.9 us
    psum x1, blocking collectives, per_device(): bias_totals = lax.psum((head_grad, hidden_grad), ('shard', 'ctx'))  21.2 us
  transfers between devices with their start and end apart: 18, of which 11 were waited for; matrix products, arithmetic and copies ran while one was open for 14% of the time, Pallas kernels for 0%

profile of v1, /device:TPU:0, one launch (start us, length us, event | category | flops | bytes accessed | tf_op | source)
XLA Modules:
  0.0 540.4 jit_solution(4045531123295723984)
XLA Ops:
  8.1 3.1 collective-permute-start
  11.2 2.1 collective-permute-start.2
  17.6 11.9 %all-gather = bf16[4,192,4]{1,2,0:T(4,128)(2,1)S(1)} all-gather(bf16[1,192,4]{1,2,0:T(4,128)(2,1)S(1)} %bitcast.183), channel_id=1, replica_groups=mesh['shard'=4,'ctx'=2,'tp'=4] {'shard'}, dimensions={0}, use_global_device_ids=true | all-gather | bytes 7680 | tf_op jit(solution)/shard_map/all_gather | solution.py:130
  29.9 26.9 %all_gather.22 = bf16[3,768,192]{2,0,1:T(4,128)(2,1)S(1)} all-gather(bf16[3,192,192]{2,0,1:T(4,128)(2,1)S(1)} %copy.29), channel_id=1, replica_groups=mesh['shard'=4,'ctx'=2,'tp'=4] {'shard'}, dimensions={1}, use_global_device_ids=true | all-gather | bytes 1105920 | tf_op jit(solution)/shard_map/all_gather | solution.py:125
  57.0 15.6 %all_gather.25 = bf16[192,768]{0,1:T(8,128)(2,1)} all-gather(bf16[192,192]{0,1:T(8,128)(2,1)S(1)} %copy.35), channel_id=1, replica_groups=mesh['shard'=4,'ctx'=2,'tp'=4] {'shard'}, dimensions={1}, use_global_device_ids=true | all-gather | bytes 368640 | tf_op jit(solution)/shard_map/all_gather | solution.py:126
  77.3 10.8 %all_gather.24 = bf16[1,1040,192]{2,0,1:T(2,128)(2,1)S(1)} all-gather(bf16[1,520,192]{2,0,1:T(2,128)(2,1)S(1)} %copy.33), channel_id=1, replica_groups=mesh['shard'=4,'ctx'=2,'tp'=4] {'ctx'}, dimensions={1}, use_global_device_ids=true | all-gather | bytes 599040 | tf_op jit(solution)/shard_map/all_gather | solution.py:151
  88.0 2.6 copy.34
  90.7 1.8 copy.31
  92.5 9.9 %all_gather.23 = bf16[1,1040,192]{2,0,1:T(2,128)(2,1)S(1)} all-gather(bf16[1,520,192]{2,0,1:T(2,128)(2,1)S(1)} %copy.31), channel_id=1, replica_groups=mesh['shard'=4,'ctx'=2,'tp'=4] {'ctx'}, dimensions={1}, use_global_device_ids=true | all-gather | bytes 599040 | tf_op jit(solution)/shard_map/all_gather | solution.py:152
  102.5 2.6 copy.32
  115.5 43.0 %all-reduce.9.cloned.1.call-done = f32[520,768]{1,0:T(8,128)} async-done(((f32[520,768]{1,0:T(8,128)}), f32[520,768]{1,0:T(8,128)}) %all-reduce.9.cloned.1.call-update) | async-done | bytes 1597456 | tf_op jit(solution)/shard_map/psum | solution.py:157
  160.6 6.9 %multiply_convert_fusion.1 = (bf16[520,768]{1,0:T(8,128)(2,1)}, f32[520,768]{1,0:T(8,128)}, f32[520,768]{1,0:T(8,128)}) fusion(f32[768]{0:T(1024)S(1)} %convert_element_type.118, bf16[768,768]{1,0:T(8,128)(2,1)} %all-gather.4.cloned.1.call-done, f32[520,768]{1,0:T(8,128)S(1)} %get-tuple-element.122, f32[768]{0:T(1024)S(1)} %get-tuple-element.100, ...), kind=kOutput, calls=%fused_computation.37 | convolution fusion | flops 641771520 | bytes 6784064 | tf_op jit(solution)/shard_map/dot_general | solution.py:162
  167.5 10.6 %all-gather.6.cloned.1.call-done = bf16[768,768]{0,1:T(8,128)(2,1)} async-done(((bf16[768,192]{0,1:T(8,128)(2,1)}), bf16[768,768]{0,1:T(8,128)(2,1)}) %all-gather.6.cloned.1.call-update) | async-done | bytes 1179664 | tf_op jit(solution)/shard_map/all_gather | solution.py:128
  178.1 3.8 convert_reduce_fusion.1
  182.8 2.0 fusion.60
  184.9 42.7 %all-reduce.13.cloned.1.call-done = f32[520,768]{1,0:T(8,128)} async-done(((f32[520,768]{1,0:T(8,128)}), f32[520,768]{1,0:T(8,128)}) %all-reduce.13.cloned.1.call-update) | async-done | bytes 1597456 | tf_op jit(solution)/shard_map/psum | solution.py:188
  227.5 2.3 multiply_reduce_fusion.1
  229.8 2.2 fusion.53
  234.2 2.5 fusion.24
  236.8 4.8 multiply_reduce_fusion
  241.6 3.7 copy.40
  245.3 2.3 copy.54
  247.6 6.0 %multiply_convert_fusion = bf16[3,520,1040]{2,1,0:T(8,128)(2,1)S(1)} fusion(f32[3,520,1040]{2,1,0:T(8,128)} %get-tuple-element.130, f32[3,520,1040]{2,1,0:T(8,128)} %copy-done, f32[3,520]{1,0:T(4,128)S(1)} %get-tuple-element.129, f32[3,520]{1,0:T(4,128)S(1)} %log_add_fusion), kind=kLoop, calls=%fused_computation.1 | loop fusion | flops 6489600 | bytes 16236480 | tf_op jit(solution)/shard_map/while/body/eval_jaxpr/convert_element_type | solution.py:85
  253.6 2.1 convolution_multiply_fusion
  255.7 3.3 copy.38
  260.3 3.4 fusion.23
  263.7 4.5 reduce-scatter.27.cloned.1.call-done
  270.5 20.4 %reduce-scatter.25.cloned.1.call-done = f32[520,192]{1,0:T(8,128)} async-done(((f32[1040,192]{1,0:T(8,128)}), f32[520,192]{1,0:T(8,128)}) %reduce-scatter.25.cloned.1.call-update) | async-done | bytes 399376
  293.7 3.4 convolution_bitcast_fusion.1
  298.1 2.9 convolution_bitcast_fusion.2
  301.1 2.4 convolution_bitcast_fusion
  303.5 4.2 copy.42
  307.7 4.7 reshape.303
  312.5 4.0 fusion.50
  316.6 4.1 fusion.41
  320.8 3.2 convolution_convert_fusion
  324.1 16.6 %all-reduce.15.cloned.1.call-done = f32[520,768]{1,0:T(8,128)} async-done(((f32[520,768]{1,0:T(8,128)}), f32[520,768]{1,0:T(8,128)}) %all-reduce.15.cloned.1.call-update) | async-done | bytes 1597456 | tf_op jit(solution)/shard_map/psum | solution.py:219
  340.7 2.2 fusion.11
  346.7 20.7 %reduce-scatter.29.cloned.1.call-done = f32[192,576]{1,0:T(8,128)} async-done(((f32[768,576]{1,0:T(8,128)}), f32[192,576]{1,0:T(8,128)}) %reduce-scatter.29.cloned.1.call-update) | async-done | bytes 442384
  369.9 46.8 %reduce-scatter.21.cloned.1.call-done = f32[192,768]{1,0:T(8,128)} async-done(((f32[768,768]{1,0:T(8,128)}), f32[192,768]{1,0:T(8,128)}) %reduce-scatter.21.cloned.1.call-update) | async-done | bytes 589840 | tf_op jit(solution)/shard_map/reduce_scatter | solution.py:243
  416.7 49.4 %reduce-scatter.23.cloned.1.call-done = f32[768,192]{0,1:T(8,128)} async-done(((f32[768,768]{0,1:T(8,128)}), f32[768,192]{0,1:T(8,128)}) %reduce-scatter.23.cloned.1.call-update) | async-done | bytes 589840 | tf_op jit(solution)/shard_map/reduce_scatter | solution.py:244
  466.7 1.8 fusion.31
  468.8 21.2 %all-reduce = (f32[2,192]{1,0:T(2,128)}, f32[768]{0:T(1024)}) all-reduce(f32[2,192]{1,0:T(2,128)S(1)} %pad_maximum_fusion.4, f32[768]{0:T(1024)S(1)} %get-tuple-element.131), channel_id=1, replica_groups=mesh['shard'=4,'ctx'=2,'tp'=4] {'shard','ctx'}, use_global_device_ids=true, to_apply=%region_38.39 | all-reduce | flops 1152 | bytes 9216 | tf_op jit(solution)/shard_map/psum | solution.py:248
  490.8 1.8 fusion.32
  493.6 17.0 %reduce-scatter.35.cloned.1.call-done = f32[192,4]{1,0:T(8,128)} async-done(((f32[768,4]{1,0:T(8,128)}), f32[192,4]{1,0:T(8,128)}) %reduce-scatter.35.cloned.1.call-update) | async-done | bytes 3088
  511.6 5.7 %all-reduce.1 = (f32[2,192]{1,0:T(2,128)}, f32[4,192]{1,0:T(4,128)}) all-reduce(f32[2,192]{1,0:T(2,128)S(1)} %copy.47, f32[4,192]{1,0:T(4,128)S(1)} %copy.49), channel_id=1, replica_groups=mesh['shard'=4,'ctx'=2,'tp'=4] {'ctx'}, use_global_device_ids=true, to_apply=%region_28.29 | all-reduce | flops 1152 | bytes 9216 | tf_op jit(solution)/shard_map/psum | solution.py:239
  517.3 10.2 %all-reduce.17.cloned.1.call-done = (f32[3,192,192]{1,2,0:T(8,128)}, f32[192,192]{1,0:T(8,128)}, f32[192,768]{1,0:T(8,128)}, f32[768,192]{0,1:T(8,128)}) async-done(((f32[3,192,192]{1,2,0:T(8,128)}, f32[192,192]{1,0:T(8,128)}, f32[192,768]{1,0:T(8,128)}, f32[768,192]{0,1:T(8,128)}), (f32[3,192,192]{1,2,0:T(8,128)}, f32[192,192]{1,0:T(8,128)}, f32[192,768]{1,0:T(8,128)}, ...) | async-done | bytes 1769488 | tf_op jit(solution)/shard_map/psum | solution.py:239
  527.5 2.2 copy.37
  (172 shorter events, 45.9 us)
Async XLA Ops:
  8.0 9.6 %copy-start.21 = (bf16[4,192]{1,0:T(4,128)(2,1)S(1)}, bf16[4,192]{1,0:T(4,128)(2,1)}, u32[]{:S(2)}) copy-start(bf16[4,192]{1,0:T(4,128)(2,1)} %param.18) | copy-start | bytes 4612
  8.0 21.6 %copy-start.18 = (bf16[3,192,192]{2,1,0:T(8,128)(2,1)S(1)}, bf16[3,192,192]{2,1,0:T(8,128)(2,1)}, u32[]{:S(2)}) copy-start(bf16[3,192,192]{2,1,0:T(8,128)(2,1)} %param.13) | copy-start | bytes 663556
  8.0 150.5 %all-reduce.9.cloned.1.call-start = ((), (), s32[]{:S(2)}) async-start(), calls=%async_computation.8 | async-start | bytes 3194880 | tf_op jit(solution)/shard_map/psum | solution.py:157
  8.1 48.9 %collective-permute-start = (bf16[2,192]{1,0:T(2,128)(2,1)}, bf16[2,192]{1,0:T(2,128)(2,1)S(1)}, u32[]{:S(2)}, u32[]{:S(2)}) collective-permute-start(bf16[2,192]{1,0:T(2,128)(2,1)} %param.17), channel_id=1, source_target_pairs={{0,8},{8,16},{16,24},{24,0},{1,9},{9,17},{17,25},{25,1},{2,10},{10... | collective-permute-start | bytes 2312 | tf_op jit(solution)/shard_map/ppermute | solution.py:25
  11.2 62.6 %collective-permute-start.2 = (bf16[2,192]{1,0:T(2,128)(2,1)}, bf16[2,192]{1,0:T(2,128)(2,1)S(1)}, u32[]{:S(2)}, u32[]{:S(2)}) collective-permute-start(bf16[2,192]{1,0:T(2,128)(2,1)} %param.17), channel_id=1, source_target_pairs={{8,0},{16,8},{24,16},{0,24},{9,1},{17,9},{25,17},{1,25},{10,2},{18... | collective-permute-start | bytes 2312 | tf_op jit(solution)/shard_map/ppermute | solution.py:27
  16.0 40.8 %copy-start.19 = (bf16[192,192]{1,0:T(8,128)(2,1)S(1)}, bf16[192,192]{1,0:T(8,128)(2,1)}, u32[]{:S(2)}) copy-start(bf16[192,192]{1,0:T(8,128)(2,1)} %param.14) | copy-start | bytes 221188
  29.6 43.0 %copy-start.20 = (bf16[2,192]{1,0:T(2,128)(2,1)S(1)}, bf16[2,192]{1,0:T(2,128)(2,1)}, u32[]{:S(2)}) copy-start(bf16[2,192]{1,0:T(2,128)(2,1)} %param.19) | copy-start | bytes 2308
  56.8 17.0 %copy-start.23 = (bf16[2,192]{1,0:T(2,128)(2,1)S(1)}, bf16[2,192]{1,0:T(2,128)(2,1)}, u32[]{:S(2)}) copy-start(bf16[2,192]{1,0:T(2,128)(2,1)} %param.17) | copy-start | bytes 2308
  56.8 17.7 %copy-start.2 = (bf16[1,520,768]{2,1,0:T(8,128)(2,1)S(1)}, bf16[1,520,768]{2,1,0:T(8,128)(2,1)}, u32[]{:S(2)}) copy-start(bf16[1,520,768]{2,1,0:T(8,128)(2,1)} %param.11) | copy-start | bytes 2396164
  56.9 16.8 %collective-permute-start.1 = (bf16[2,192]{1,0:T(2,128)(2,1)S(1)}, bf16[2,192]{1,0:T(2,128)(2,1)S(1)}, u32[]{:S(2)}, u32[]{:S(2)}) collective-permute-start(bf16[2,192]{1,0:T(2,128)(2,1)S(1)} %collective-permute-done), channel_id=1, source_target_pairs={{0,8},{8,16},{16,24},{24,0},{1,9},{9,17},{17,25},{25,1},{2,10},{10... | collective-permute-start | bytes 2312 | tf_op jit(solution)/shard_map/ppermute | solution.py:25
  73.7 1.8 copy-start.14
  90.7 14.4 %copy-start.5 = (bf16[1,1040,192]{1,2,0:T(8,128)(2,1)}, bf16[1,1040,192]{1,2,0:T(8,128)(2,1)S(1)}, u32[]{:S(2)}) copy-start(bf16[1,1040,192]{1,2,0:T(8,128)(2,1)S(1)} %copy.34) | copy-start | bytes 1198084
  106.6 3.0 copy-start
  109.6 1.4 copy-start.6
  111.0 1.7 copy-start.8
  112.7 1.4 copy-start.24
  112.7 2.7 copy-start.22
  112.7 47.9 %all-gather.4.cloned.1.call-start = ((), (), s32[]{:S(2)}) async-start(), calls=%async_computation.9 | async-start | bytes 1474560 | tf_op jit(solution)/shard_map/all_gather | solution.py:127
  113.3 64.8 %all-gather.6.cloned.1.call-start = ((), (), s32[]{:S(2)}) async-start(), calls=%async_computation.10 | async-start | bytes 1474560 | tf_op jit(solution)/shard_map/all_gather | solution.py:128
  113.9 113.7 %all-reduce.13.cloned.1.call-start = ((), (), s32[]{:S(2)}) async-start(), calls=%async_computation.12 | async-start | bytes 3194880 | tf_op jit(solution)/shard_map/psum | solution.py:188
  178.1 4.7 copy-start.25
  181.9 0.9 copy-start.26
  184.8 83.4 %reduce-scatter.27.cloned.1.call-start = ((), (), s32[]{:S(2)}) async-start(), calls=%async_computation.17 | async-start | bytes 1597440
  227.5 6.7 %slice-start = ((s8[7188480]{0:T(1024)(128)(4,1)}), s8[4194304]{0:T(1024)(128)(4,1)S(1)}, s32[]{:S(2)}) async-start(s8[7188480]{0:T(1024)(128)(4,1)} %bitcast.148), calls=%async_computation.23 | async-start | bytes 8388608
  229.8 2.3 copy-start.15
  229.8 4.4 slice-start.1
  232.1 1.6 copy-start.7
  232.5 1.2 copy-start.3
  247.6 43.4 %reduce-scatter.25.cloned.1.call-start = ((), (), s32[]{:S(2)}) async-start(), calls=%async_computation.16 | async-start | bytes 1597440
  253.6 2.1 copy-start.1
  260.1 80.6 %all-reduce.15.cloned.1.call-start = ((), (), s32[]{:S(2)}) async-start(), calls=%async_computation.13 | async-start | bytes 3194880 | tf_op jit(solution)/shard_map/psum | solution.py:219
  270.5 30.5 %copy-start.10 = (bf16[1,520,192]{1,2,0:T(8,128)(2,1)}, bf16[1,520,192]{1,2,0:T(8,128)(2,1)S(1)}, u32[]{:S(2)}) copy-start(bf16[1,520,192]{1,2,0:T(8,128)(2,1)S(1)} %copy.41) | copy-start | bytes 599044
  297.1 0.9 copy-start.9
  297.2 3.9 copy-start.12
  297.2 47.8 %reduce-scatter.31.cloned.1.call-start = ((), (), s32[]{:S(2)}) async-start(), calls=%async_computation.19 | async-start | bytes 983040
  301.0 66.4 %reduce-scatter.29.cloned.1.call-start = ((), (), s32[]{:S(2)}) async-start(), calls=%async_computation.18 | async-start | bytes 2457600
  312.4 104.2 %reduce-scatter.21.cloned.1.call-start = ((), (), s32[]{:S(2)}) async-start(), calls=%async_computation.14 | async-start | bytes 2949120 | tf_op jit(solution)/shard_map/reduce_scatter | solution.py:243
  316.6 149.5 %reduce-scatter.23.cloned.1.call-start = ((), (), s32[]{:S(2)}) async-start(), calls=%async_computation.15 | async-start | bytes 2949120 | tf_op jit(solution)/shard_map/reduce_scatter | solution.py:244
  320.7 146.0 %all-reduce.11.cloned.1.call-start = ((), (), s32[]{:S(2)}) async-start(), calls=%async_computation.11 | async-start | bytes 1597440 | tf_op jit(solution)/shard_map/psum | solution.py:168
  324.0 168.6 %reduce-scatter.33.cloned.1.call-start = ((), (), s32[]{:S(2)}) async-start(), calls=%async_computation.20 | async-start | bytes 491520
  343.9 166.7 %reduce-scatter.35.cloned.1.call-start = ((), (), s32[]{:S(2)}) async-start(), calls=%async_computation.21 | async-start | bytes 491520
  344.9 182.5 %all-reduce.17.cloned.1.call-start = ((), (), s32[]{:S(2)}) async-start(), calls=%async_computation.22 | async-start | bytes 3932160 | tf_op jit(solution)/shard_map/psum | solution.py:239
  369.9 98.6 %copy-start.11 = (bf16[1,520,192]{1,2,0:T(8,128)(2,1)S(1)}, bf16[1,520,192]{1,2,0:T(8,128)(2,1)}, u32[]{:S(2)}) copy-start(bf16[1,520,192]{1,2,0:T(8,128)(2,1)} %copy-done.10) | copy-start | bytes 599044
  369.9 98.6 %copy-start.13 = (bf16[1,520,192]{1,2,0:T(8,128)(2,1)S(1)}, bf16[1,520,192]{1,2,0:T(8,128)(2,1)}, u32[]{:S(2)}) copy-start(bf16[1,520,192]{1,2,0:T(8,128)(2,1)} %copy.39) | copy-start | bytes 599044
  468.5 21.5 %copy-start.4 = (f32[520,768]{1,0:T(8,128)S(1)}, f32[520,768]{1,0:T(8,128)}, u32[]{:S(2)}) copy-start(f32[520,768]{1,0:T(8,128)} %all-reduce.15.cloned.1.call-done) | copy-start | bytes 4792324
  527.5 3.8 copy-start.17
  527.5 4.7 copy-start.16
Sparse Core Ops, SparseCore 0:
  112.8 45.6 all-reduce.8
  185.0 42.5 all-reduce.12
  247.7 20.4 reduce-scatter.26
  270.4 20.4 reduce-scatter.24
  297.3 43.3 all-reduce.14
  342.9 34.5 all-reduce.10
  466.2 61.2 all-reduce.16
Sparse Core Ops, SparseCore 1:
  114.7 32.5 all-gather.3
  148.7 29.4 all-gather.5
  301.1 23.0 reduce-scatter.30
  326.5 40.9 reduce-scatter.28
  369.7 46.9 reduce-scatter.20
  419.0 47.0 reduce-scatter.22
  468.8 19.8 reduce-scatter.32
  491.4 19.1 reduce-scatter.34
